TPU v7x, 256 devices: a whole 4x4x8 slice. The times are simulated.
256 devices in a mesh: tm: 32 (over z, y_lo, core), gz: 8 (over y_hi, x).
Axes of the slice: x: 4, y: 4 (y_hi: 2, y_lo: 2; y = y_hi * 2 + y_lo), z: 8, core: 2. Of those that a mesh axis runs over, the one named last changes fastest.
Arguments:
- states: float32 [32, 4, 32, 128, 128], P('tm', None, 'gz'), may hold values from -6 to 6
- first_unconverged: int32 [1], replicated, may hold values from 0 to 31
- window_offset: int32 [1], replicated, may hold values from 0 to 63
- summaries: float32 [64], replicated, may hold values from -5 to 5
- cond_weight: float32 [64, 32], replicated, may hold values from -0.75 to 0.75
- time_gain: float32 [32], replicated, may hold values from -4 to 4
- conv_weight: float32 [27, 32, 4], replicated, may hold values from -0.625 to 0.625
- out_weight: float32 [4, 32], replicated, may hold values from -1 to 1
Outputs:
- new_states: float32 [32, 4, 32, 128, 128], P('tm', None, 'gz')
All inputs are finite; a program needn't handle non-finite values.
Results may differ from a plain program's by a relative error of at most 0.0001.
Values sent between devices are 32-bit elements; how exact they have to be, the bound alone decides.
A program may use at most 128 MiB of HBM per device.

v0:
```python
import jax
import jax.numpy as jnp
from jax import lax
from jax.sharding import PartitionSpec as P

STEP_SIZE = 0.125


def extended(block, sides, width):
    for axis, dim in sides:
        count = lax.axis_size(axis)
        forward = [(i, i + 1) for i in range(count - 1)]
        forward.append((count - 1, 0))
        backward = [(target, source) for source, target in forward]
        low = lax.ppermute(
            lax.slice_in_dim(block, block.shape[dim] - width, None, axis=dim), axis, forward
        )
        high = lax.ppermute(lax.slice_in_dim(block, 0, width, axis=dim), axis, backward)
        block = jnp.concatenate([low, block, high], axis=dim)
    return block


def carried_in(shard, axis, combine, identity):
    size, place = (lax.axis_size(axis), lax.axis_index(axis))
    everything = lax.all_gather(shard, axis)
    start = jnp.broadcast_to(jnp.asarray(identity, shard.dtype), shard.shape)

    def hop(k, before):
        reached = k < place
        new = combine(before, everything[k])
        return jnp.where(reached, new, before)

    return lax.fori_loop(0, size, hop, start)


def spread(shard, axis, root):
    mine = lax.axis_index(axis) == root
    return lax.psum(jnp.where(mine, shard, jnp.zeros_like(shard)), axis)


def shards(
    states,
    first_unconverged,
    window_offset,
    summaries,
    cond_weight,
    time_gain,
    conv_weight,
    out_weight,
):
    local_steps = states.shape[0]
    channels = states.shape[1]
    planes = states.shape[2]
    rows_y = states.shape[3]
    cols_x = states.shape[4]
    hidden_width = conv_weight.shape[1]
    all_steps = local_steps * lax.axis_size("tm")
    my_index = lax.axis_index("tm")
    global_steps = my_index * local_steps + jnp.arange(local_steps, dtype=jnp.int32)
    step_times = 1.0 - (window_offset[0] + global_steps).astype(jnp.float32) / float(all_steps + 64)
    condition = jnp.dot(
        summaries, cond_weight, precision=lax.Precision.HIGHEST, preferred_element_type=jnp.float32
    )
    stacked_weight = jnp.transpose(conv_weight, (1, 0, 2)).reshape(hidden_width, 27 * channels)
    padded = extended(states, (("gz", 2),), 1)

    def one_step(pair_item):
        state_block, step_time = pair_item
        offset_term = condition + step_time * time_gain

        def one_plane(plane_index):
            window_slab = lax.dynamic_slice_in_dim(state_block, plane_index, 3, 1)
            pieces = []
            for shift_z in (-1, 0, 1):
                for shift_y in (-1, 0, 1):
                    for shift_x in (-1, 0, 1):
                        pieces.append(
                            jnp.roll(window_slab[:, shift_z + 1], (-shift_y, -shift_x), axis=(1, 2))
                        )
            stacked = jnp.concatenate(pieces, axis=0).reshape(27 * channels, rows_y * cols_x)
            hidden = jnp.dot(
                stacked_weight,
                stacked,
                precision=lax.Precision.HIGHEST,
                preferred_element_type=jnp.float32,
            )
            activation = jax.nn.silu(hidden + offset_term[:, None])
            drift_plane = STEP_SIZE * jnp.dot(
                out_weight,
                activation,
                precision=lax.Precision.HIGHEST,
                preferred_element_type=jnp.float32,
            )
            return drift_plane.reshape(channels, rows_y, cols_x)

        drift_term = lax.map(one_plane, jnp.arange(planes, dtype=jnp.int32))
        return jnp.transpose(drift_term, (1, 0, 2, 3))

    increments = lax.map(one_step, (padded, step_times))
    running = jnp.cumsum(increments, axis=0)
    local_before = running - increments
    earlier_sum = carried_in(
        running[-1], "tm", lambda earlier, later: earlier + later, jnp.zeros_like(running[-1])
    )
    prefix = earlier_sum[None] + local_before
    root_device = first_unconverged[0] // local_steps
    local_row = first_unconverged[0] % local_steps
    picked = lax.dynamic_index_in_dim(states, local_row, 0, keepdims=False)
    anchor = spread(picked, "tm", root_device)
    return anchor[None] + prefix


def solution(mesh):
    placed = (P("tm", None, "gz", None, None), P(), P(), P(), P(), P(), P(), P())
    return jax.shard_map(
        shards,
        mesh=mesh,
        in_specs=placed,
        out_specs=P("tm", None, "gz", None, None),
        check_vma=False,
    )
```

profile of v0, /device:TPU:1, one launch (start us, length us, event | category | flops | bytes accessed | tf_op | source)
XLA Modules:
  0.0 662.2 jit_solution(2371562767231627077)
XLA Ops:
  7.6 2.1 collective-permute-start
  9.8 4.0 collective-permute-start.1
  18.8 213.9 %while.31 = (s32[]{:T(128)}, f32[4,4,128,128]{3,2,0,1:T(8,128)}, s32[4]{0:T(128)S(1)}, f32[4,6,128,128]{3,2,1,0:T(8,128)S(1)}, f32[32,108]{1,0:T(8,128)S(1)}, /*...) while((s32[]{:T(128)}, f32[4,4,128,128]{3,2,0,1:T(8,128)}, ...), condition=%wide.region_2.3_spmd, body=%wide.region_1.2_spmd.sunk | while | flops 709689344 | bytes 80493440 | solution.py:96
  40.6 22.0 %concatenate.159 = f32[108,16384]{1,0:T(8,128)} concatenate(f32[4,16384]{1,0:T(4,128)} %bitcast.325, f32[4,16384]{1,0:T(4,128)} %bitcast.323, f32[4,16384]{1,0:T(4,128)} %bitcast.322, f32[4,16384]{1,0:T(4,128)} %bitcast.320, f32[4,16384]{1,0:T(4,128)} %bitcast.326, f32[4,16384]{1,0:T(4,128)} %bitcast.321, f32[4,16384]{1,0:T(4,128)} %bitcast.318, f32[4,16384]{1,0:T(4,128)} %bitcast.324, ...), dimensions={0} | concatenate | bytes 14155776 | tf_op jit(solution)/shard_map/while/body/eval_jaxpr/while/body/eval_jaxpr/concatenate | solution.py:80
  62.7 7.2 %fusion.118 = f32[32,16384]{1,0:T(8,128)S(1)} fusion(f32[108,16384]{1,0:T(8,128)} %concatenate.159, f32[32,108]{1,0:T(8,128)S(1)} %get-tuple-element.488, f32[32]{0:T(128)S(1)} %get-tuple-element.489), kind=kOutput, calls=%fused_computation.1.clone.1 | convolution fusion | flops 680001536 | bytes 9188992 | tf_op jit(solution)/shard_map/while/body/eval_jaxpr/while/body/eval_jaxpr/dot_general | solution.py:81
  69.9 1.6 fusion.119
  94.1 22.0 %concatenate.159 = f32[108,16384]{1,0:T(8,128)} concatenate(f32[4,16384]{1,0:T(4,128)} %bitcast.325, f32[4,16384]{1,0:T(4,128)} %bitcast.323, f32[4,16384]{1,0:T(4,128)} %bitcast.322, f32[4,16384]{1,0:T(4,128)} %bitcast.320, f32[4,16384]{1,0:T(4,128)} %bitcast.326, f32[4,16384]{1,0:T(4,128)} %bitcast.321, f32[4,16384]{1,0:T(4,128)} %bitcast.318, f32[4,16384]{1,0:T(4,128)} %bitcast.324, ...), dimensions={0} | concatenate | bytes 14155776 | tf_op jit(solution)/shard_map/while/body/eval_jaxpr/while/body/eval_jaxpr/concatenate | solution.py:80
  116.1 7.2 %fusion.118 = f32[32,16384]{1,0:T(8,128)S(1)} fusion(f32[108,16384]{1,0:T(8,128)} %concatenate.159, f32[32,108]{1,0:T(8,128)S(1)} %get-tuple-element.488, f32[32]{0:T(128)S(1)} %get-tuple-element.489), kind=kOutput, calls=%fused_computation.1.clone.1 | convolution fusion | flops 680001536 | bytes 9188992 | tf_op jit(solution)/shard_map/while/body/eval_jaxpr/while/body/eval_jaxpr/dot_general | solution.py:81
  123.3 1.6 fusion.119
  147.6 22.0 %concatenate.159 = f32[108,16384]{1,0:T(8,128)} concatenate(f32[4,16384]{1,0:T(4,128)} %bitcast.325, f32[4,16384]{1,0:T(4,128)} %bitcast.323, f32[4,16384]{1,0:T(4,128)} %bitcast.322, f32[4,16384]{1,0:T(4,128)} %bitcast.320, f32[4,16384]{1,0:T(4,128)} %bitcast.326, f32[4,16384]{1,0:T(4,128)} %bitcast.321, f32[4,16384]{1,0:T(4,128)} %bitcast.318, f32[4,16384]{1,0:T(4,128)} %bitcast.324, ...), dimensions={0} | concatenate | bytes 14155776 | tf_op jit(solution)/shard_map/while/body/eval_jaxpr/while/body/eval_jaxpr/concatenate | solution.py:80
  169.6 7.2 %fusion.118 = f32[32,16384]{1,0:T(8,128)S(1)} fusion(f32[108,16384]{1,0:T(8,128)} %concatenate.159, f32[32,108]{1,0:T(8,128)S(1)} %get-tuple-element.488, f32[32]{0:T(128)S(1)} %get-tuple-element.489), kind=kOutput, calls=%fused_computation.1.clone.1 | convolution fusion | flops 680001536 | bytes 9188992 | tf_op jit(solution)/shard_map/while/body/eval_jaxpr/while/body/eval_jaxpr/dot_general | solution.py:81
  176.8 1.6 fusion.119
  201.0 22.0 %concatenate.159 = f32[108,16384]{1,0:T(8,128)} concatenate(f32[4,16384]{1,0:T(4,128)} %bitcast.325, f32[4,16384]{1,0:T(4,128)} %bitcast.323, f32[4,16384]{1,0:T(4,128)} %bitcast.322, f32[4,16384]{1,0:T(4,128)} %bitcast.320, f32[4,16384]{1,0:T(4,128)} %bitcast.326, f32[4,16384]{1,0:T(4,128)} %bitcast.321, f32[4,16384]{1,0:T(4,128)} %bitcast.318, f32[4,16384]{1,0:T(4,128)} %bitcast.324, ...), dimensions={0} | concatenate | bytes 14155776 | tf_op jit(solution)/shard_map/while/body/eval_jaxpr/while/body/eval_jaxpr/concatenate | solution.py:80
  223.0 7.2 %fusion.118 = f32[32,16384]{1,0:T(8,128)S(1)} fusion(f32[108,16384]{1,0:T(8,128)} %concatenate.159, f32[32,108]{1,0:T(8,128)S(1)} %get-tuple-element.488, f32[32]{0:T(128)S(1)} %get-tuple-element.489), kind=kOutput, calls=%fused_computation.1.clone.1 | convolution fusion | flops 680001536 | bytes 9188992 | tf_op jit(solution)/shard_map/while/body/eval_jaxpr/while/body/eval_jaxpr/dot_general | solution.py:81
  230.3 1.6 fusion.119
  234.5 189.1 %all-gather.3.cloned.1.call-done = f32[128,4,128,128]{3,2,1,0:T(8,128)} async-done(((f32[4,4,128,128]{3,2,1,0:T(8,128)}), f32[128,4,128,128]{3,2,1,0:T(8,128)}) %all-gather.3.cloned.1.call-update) | async-done | bytes 33554448 | tf_op jit(solution)/shard_map/all_gather | solution.py:25
  423.6 51.8 %while.32 = (s32[]{:T(128)}, f32[4,4,128,128]{3,2,1,0:T(8,128)S(1)}, s32[]{:T(128)}, f32[32,4,4,128,128]{4,3,2,1,0:T(8,128)}, s32[]{:T(128)}, /*index=5*/s32[]{:T(128)}) while((s32[]{:T(128)}, f32[4,4,128,128]{3,2,1,0:T(8,128)S(1)}, s32[]{:T(128)}, f32[32,4,4,128,128]{4,3,2,1,0:T(8,128)}, s32[]{:T(128)}, ...), condition=%wide.region_4.5_spmd.clone, body=%wide.region_3.4_spmd.clone.sunk | while | flops 786436 | bytes 3145821 | solution.py:33
  423.6 1.7 add_select_fusion.2
  425.3 1.6 add_select_fusion.2
  426.9 1.6 add_select_fusion.2
  428.5 1.6 add_select_fusion.2
  430.1 1.6 add_select_fusion.2
  431.7 1.6 add_select_fusion.2
  433.4 1.6 add_select_fusion.2
  435.0 1.6 add_select_fusion.2
  436.6 1.6 add_select_fusion.2
  438.2 1.6 add_select_fusion.2
  439.8 1.6 add_select_fusion.2
  441.4 1.6 add_select_fusion.2
  443.1 1.6 add_select_fusion.2
  444.7 1.6 add_select_fusion.2
  446.3 1.6 add_select_fusion.2
  447.9 1.6 add_select_fusion.2
  449.5 1.6 add_select_fusion.2
  451.1 1.6 add_select_fusion.2
  452.8 1.6 add_select_fusion.2
  454.4 1.6 add_select_fusion.2
  456.0 1.6 add_select_fusion.2
  457.6 1.6 add_select_fusion.2
  459.2 1.6 add_select_fusion.2
  460.8 1.6 add_select_fusion.2
  464.1 1.6 add_select_fusion.2
  465.7 1.6 add_select_fusion.2
  467.3 1.6 add_select_fusion.2
  470.5 1.6 add_select_fusion.2
  472.2 1.6 add_select_fusion.2
  475.4 177.5 %all-reduce.2.cloned.1.call-done = f32[4,4,128,128]{3,2,1,0:T(8,128)} async-done(((f32[4,4,128,128]{3,2,1,0:T(8,128)}), f32[4,4,128,128]{3,2,1,0:T(8,128)}) %all-reduce.2.cloned.1.call-update) | async-done | bytes 1048592 | tf_op jit(solution)/shard_map/psum | solution.py:38
  652.9 2.4 add_bitcast_fusion
  (318 shorter events, 92.7 us)
Async XLA Ops:
  6.5 8.8 %copy-start = (f32[64,32]{0,1:T(8,128)S(1)}, f32[64,32]{0,1:T(8,128)}, u32[]{:S(2)}) copy-start(f32[64,32]{0,1:T(8,128)} %param.16) | copy-start | bytes 24580
  6.5 12.2 %copy-start.5 = (f32[4,32]{1,0:T(4,128)S(1)}, f32[4,32]{1,0:T(4,128)}, u32[]{:S(2)}) copy-start(f32[4,32]{1,0:T(4,128)} %param.19) | copy-start | bytes 1540
  6.5 417.0 %all-gather.3.cloned.1.call-start = ((), (), s32[]{:S(2)}) async-start(), calls=%async_computation.1 | async-start | bytes 34603008 | tf_op jit(solution)/shard_map/all_gather | solution.py:25
  7.6 9.8 %collective-permute-start = (f32[1,4,1,128,128]{4,3,2,1,0:T(8,128)S(1)}, f32[1,4,1,128,128]{4,3,2,1,0:T(8,128)S(1)}, u32[]{:S(2)}, u32[]{:S(2)}) collective-permute-start(f32[1,4,1,128,128]{4,3,2,1,0:T(8,128)S(1)} %get-tuple-element.270), channel_id=1, source_target_pairs={{0,1},{1,2},{2,3},{3,4},{4,5},{5,6},{6,7},{7,0},{8,9},{9,10},{10,1... | collective-permute-start | bytes 786440 | tf_op jit(solution)/shard_map/ppermute | solution.py:15
  9.8 7.7 %collective-permute-start.1 = (f32[1,4,1,128,128]{4,3,2,1,0:T(8,128)S(1)}, f32[1,4,1,128,128]{4,3,2,1,0:T(8,128)S(1)}, u32[]{:S(2)}, u32[]{:S(2)}) collective-permute-start(f32[1,4,1,128,128]{4,3,2,1,0:T(8,128)S(1)} %get-tuple-element.271), channel_id=1, source_target_pairs={{1,0},{2,1},{3,2},{4,3},{5,4},{6,5},{7,6},{0,7},{9,8},{10,9},{11,1... | collective-permute-start | bytes 786440 | tf_op jit(solution)/shard_map/ppermute | solution.py:18
  18.8 2.9 copy-start.2
  69.9 2.4 copy-start.3
  72.3 2.9 copy-start.2
  123.3 2.4 copy-start.3
  125.7 2.9 copy-start.2
  176.8 2.4 copy-start.3
  179.2 2.9 copy-start.2
  230.3 2.4 copy-start.3
  232.7 420.3 %all-reduce.2.cloned.1.call-start = ((), (), s32[]{:S(2)}) async-start(), calls=%async_computation | async-start | bytes 2097152 | tf_op jit(solution)/shard_map/psum | solution.py:38
  423.6 229.3 %copy-start.4 = (f32[4,4,128,128]{3,2,0,1:T(8,128)S(1)}, f32[4,4,128,128]{3,2,0,1:T(8,128)}, u32[]{:S(2)}) copy-start(f32[4,4,128,128]{3,2,0,1:T(8,128)} %get-tuple-element.145) | copy-start | bytes 3145732
  652.9 2.4 copy-start.1
Sparse Core Ops, SparseCore 0:
  232.8 190.7 all-gather.2
  426.2 226.6 all-reduce.1
where the time goes:
time: 665 us; the launch traced here: 662 us
  waiting for transfers between devices  368 us (55%)
  local copies, waits for them, and re-layouts  155 us (23%)
  other arithmetic  72.2 us (11%)
  matrix products  36.1 us (5%)
  between operations  14.8 us (2%)
  loops' own time  9.96 us (1%)
    all_gather x1, waiting for transfers between devices, carried_in(): everything = lax.all_gather(shard, axis)  189 us
    psum x1, waiting for transfers between devices, spread(): return lax.psum(jnp.where(mine, shard, jnp.zeros_like(shard)), axis)  178 us
    concatenate x8, local copies, waits for them, and re-layouts, one_plane(): jnp.concatenate(pieces, axis=0).reshape(27 * channels, rows_y * cols_x)  92.5 us
    while x120, local copies, waits for them, and re-layouts  51.6 us
    select_n x32, other arithmetic, hop(): return jnp.where(reached, new, before)  51 us
    dot_general x4, matrix products, one_plane(): jnp.dot(stacked_weight, stacked, precision=lax.Precision.HIGHEST, preferr...  28.8 us
  transfers between devices with their start and end apart: 4, of which 3 were waited for; matrix products, arithmetic and copies ran while one was open for 8% of the time, Pallas kernels for 0%

commit v1 on v0

--- a/solution.py
+++ b/solution.py
@@ -35,7 +35,7 @@
 
 def spread(shard, axis, root):
     mine = lax.axis_index(axis) == root
-    return lax.psum(jnp.where(mine, shard, jnp.zeros_like(shard)), axis)
+    return jnp.sum(lax.all_gather(jnp.where(mine, shard, jnp.zeros_like(shard)), axis), axis=0)
 
 
 def shards(

time: 665 us -> 487 us (0.73)
  waiting for transfers between devices: 368 us -> 182 us
  other arithmetic: 72.2 us -> 81.4 us
    psum x1 -> x0, waiting for transfers between devices: 178 us -> none  [spread(): return lax.psum(jnp.where(mine, shard, jnp.zeros_like(shard)), axis)]
    reduce_sum x0 -> x1, other arithmetic: none -> 11.7 us  [spread(): jnp.sum(lax.all_gather(jnp.where(mine, shard, jnp.zeros_like(shard)), axi...]
    all_gather x1, waiting for transfers between devices: 189 us -> 179 us  [carried_in(): everything = lax.all_gather(shard, axis)]
  transfers between devices with their start and end apart: 4 -> 4, of which waited for: 3 -> 2; matrix products, arithmetic and copies ran while one was open for 8% -> 45% of each run, Pallas kernels for 0% -> 0%
where the time goes in v1:
time: 487 us; the launch traced here: 484 us
  waiting for transfers between devices  182 us (37%)
  local copies, waits for them, and re-layouts  154 us (32%)
  other arithmetic  81.4 us (17%)
  matrix products  35.7 us (7%)
  between operations  15 us (3%)
  loops' own time  9.75 us (2%)
  starting transfers between devices  6.15 us (1%)
    all_gather x1, waiting for transfers between devices, carried_in(): everything = lax.all_gather(shard, axis)  179 us
    concatenate x8, local copies, waits for them, and re-layouts, one_plane(): jnp.concatenate(pieces, axis=0).reshape(27 * channels, rows_y * cols_x)  93 us
    while x120, local copies, waits for them, and re-layouts  51.8 us
    select_n x32, other arithmetic, hop(): return jnp.where(reached, new, before)  50.9 us
    dot_general x4, matrix products, one_plane(): jnp.dot(stacked_weight, stacked, precision=lax.Precision.HIGHEST, preferr...  29.1 us
    reduce_sum x1, other arithmetic, spread(): jnp.sum(lax.all_gather(jnp.where(mine, shard, jnp.zeros_like(shard)), axi...  11.7 us
    while x88, other arithmetic  10.1 us
  transfers between devices with their start and end apart: 4, of which 2 were waited for; matrix products, arithmetic and copies ran while one was open for 45% of the time, Pallas kernels for 0%

profile of v1, /device:TPU:1, one launch (start us, length us, event | category | flops | bytes accessed | tf_op | source)
XLA Modules:
  0.0 484.3 jit_solution(14228981428845207275)
XLA Ops:
  8.5 2.1 collective-permute-start
  10.7 4.0 collective-permute-start.1
  15.6 2.8 collective-permute-done
  18.5 215.0 %while.31 = (s32[]{:T(128)}, f32[4,4,128,128]{3,2,0,1:T(8,128)}, s32[4]{0:T(128)S(1)}, f32[4,6,128,128]{3,2,1,0:T(8,128)S(1)}, f32[32,108]{1,0:T(8,128)S(1)}, /*...) while((s32[]{:T(128)}, f32[4,4,128,128]{3,2,0,1:T(8,128)}, ...), condition=%wide.region_2.3_spmd, body=%wide.region_1.2_spmd.sunk | while | flops 709689344 | bytes 80493440 | solution.py:96
  40.5 22.2 %concatenate.159 = f32[108,16384]{1,0:T(8,128)} concatenate(f32[4,16384]{1,0:T(4,128)} %bitcast.323, f32[4,16384]{1,0:T(4,128)} %bitcast.321, f32[4,16384]{1,0:T(4,128)} %bitcast.320, f32[4,16384]{1,0:T(4,128)} %bitcast.318, f32[4,16384]{1,0:T(4,128)} %bitcast.324, f32[4,16384]{1,0:T(4,128)} %bitcast.319, f32[4,16384]{1,0:T(4,128)} %bitcast.316, f32[4,16384]{1,0:T(4,128)} %bitcast.322, ...), dimensions={0} | concatenate | bytes 14155776 | tf_op jit(solution)/shard_map/while/body/eval_jaxpr/while/body/eval_jaxpr/concatenate | solution.py:80
  62.6 7.2 %fusion.118 = f32[32,16384]{1,0:T(8,128)S(1)} fusion(f32[108,16384]{1,0:T(8,128)} %concatenate.159, f32[32,108]{1,0:T(8,128)S(1)} %get-tuple-element.488, f32[32]{0:T(128)S(1)} %get-tuple-element.489), kind=kOutput, calls=%fused_computation.1.clone.1 | convolution fusion | flops 680001536 | bytes 9188992 | tf_op jit(solution)/shard_map/while/body/eval_jaxpr/while/body/eval_jaxpr/dot_general | solution.py:81
  69.9 1.6 fusion.119
  94.2 22.0 %concatenate.159 = f32[108,16384]{1,0:T(8,128)} concatenate(f32[4,16384]{1,0:T(4,128)} %bitcast.323, f32[4,16384]{1,0:T(4,128)} %bitcast.321, f32[4,16384]{1,0:T(4,128)} %bitcast.320, f32[4,16384]{1,0:T(4,128)} %bitcast.318, f32[4,16384]{1,0:T(4,128)} %bitcast.324, f32[4,16384]{1,0:T(4,128)} %bitcast.319, f32[4,16384]{1,0:T(4,128)} %bitcast.316, f32[4,16384]{1,0:T(4,128)} %bitcast.322, ...), dimensions={0} | concatenate | bytes 14155776 | tf_op jit(solution)/shard_map/while/body/eval_jaxpr/while/body/eval_jaxpr/concatenate | solution.py:80
  116.3 7.3 %fusion.118 = f32[32,16384]{1,0:T(8,128)S(1)} fusion(f32[108,16384]{1,0:T(8,128)} %concatenate.159, f32[32,108]{1,0:T(8,128)S(1)} %get-tuple-element.488, f32[32]{0:T(128)S(1)} %get-tuple-element.489), kind=kOutput, calls=%fused_computation.1.clone.1 | convolution fusion | flops 680001536 | bytes 9188992 | tf_op jit(solution)/shard_map/while/body/eval_jaxpr/while/body/eval_jaxpr/dot_general | solution.py:81
  123.6 1.6 fusion.119
  147.9 22.2 %concatenate.159 = f32[108,16384]{1,0:T(8,128)} concatenate(f32[4,16384]{1,0:T(4,128)} %bitcast.323, f32[4,16384]{1,0:T(4,128)} %bitcast.321, f32[4,16384]{1,0:T(4,128)} %bitcast.320, f32[4,16384]{1,0:T(4,128)} %bitcast.318, f32[4,16384]{1,0:T(4,128)} %bitcast.324, f32[4,16384]{1,0:T(4,128)} %bitcast.319, f32[4,16384]{1,0:T(4,128)} %bitcast.316, f32[4,16384]{1,0:T(4,128)} %bitcast.322, ...), dimensions={0} | concatenate | bytes 14155776 | tf_op jit(solution)/shard_map/while/body/eval_jaxpr/while/body/eval_jaxpr/concatenate | solution.py:80
  170.1 7.4 %fusion.118 = f32[32,16384]{1,0:T(8,128)S(1)} fusion(f32[108,16384]{1,0:T(8,128)} %concatenate.159, f32[32,108]{1,0:T(8,128)S(1)} %get-tuple-element.488, f32[32]{0:T(128)S(1)} %get-tuple-element.489), kind=kOutput, calls=%fused_computation.1.clone.1 | convolution fusion | flops 680001536 | bytes 9188992 | tf_op jit(solution)/shard_map/while/body/eval_jaxpr/while/body/eval_jaxpr/dot_general | solution.py:81
  177.5 1.6 fusion.119
  201.8 22.0 %concatenate.159 = f32[108,16384]{1,0:T(8,128)} concatenate(f32[4,16384]{1,0:T(4,128)} %bitcast.323, f32[4,16384]{1,0:T(4,128)} %bitcast.321, f32[4,16384]{1,0:T(4,128)} %bitcast.320, f32[4,16384]{1,0:T(4,128)} %bitcast.318, f32[4,16384]{1,0:T(4,128)} %bitcast.324, f32[4,16384]{1,0:T(4,128)} %bitcast.319, f32[4,16384]{1,0:T(4,128)} %bitcast.316, f32[4,16384]{1,0:T(4,128)} %bitcast.322, ...), dimensions={0} | concatenate | bytes 14155776 | tf_op jit(solution)/shard_map/while/body/eval_jaxpr/while/body/eval_jaxpr/concatenate | solution.py:80
  223.8 7.2 %fusion.118 = f32[32,16384]{1,0:T(8,128)S(1)} fusion(f32[108,16384]{1,0:T(8,128)} %concatenate.159, f32[32,108]{1,0:T(8,128)S(1)} %get-tuple-element.488, f32[32]{0:T(128)S(1)} %get-tuple-element.489), kind=kOutput, calls=%fused_computation.1.clone.1 | convolution fusion | flops 680001536 | bytes 9188992 | tf_op jit(solution)/shard_map/while/body/eval_jaxpr/while/body/eval_jaxpr/dot_general | solution.py:81
  231.1 1.6 fusion.119
  233.5 11.7 %reduce_sum.9 = f32[4,4,128,128]{3,2,1,0:T(8,128)S(1)} reduce(f32[32,4,4,128,128]{4,3,2,1,0:T(8,128)} %all-gather.4.cloned.1.call-done, f32[]{:T(128)} %constant.86.clone.1), dimensions={0}, to_apply=%region_0.1 | reduce | flops 8126464 | bytes 34603012 | tf_op jit(solution)/shard_map/reduce_sum | solution.py:38
  245.2 179.3 %all-gather.6.cloned.1.call-done = f32[128,4,128,128]{3,2,1,0:T(8,128)} async-done(((f32[4,4,128,128]{3,2,1,0:T(8,128)}), f32[128,4,128,128]{3,2,1,0:T(8,128)}) %all-gather.6.cloned.1.call-update) | async-done | bytes 33554448 | tf_op jit(solution)/shard_map/all_gather | solution.py:25
  424.5 51.7 %while.32 = (s32[]{:T(128)}, f32[4,4,128,128]{3,2,1,0:T(8,128)S(1)}, s32[]{:T(128)}, f32[32,4,4,128,128]{4,3,2,1,0:T(8,128)}, s32[]{:T(128)}, /*index=5*/s32[]{:T(128)}) while((s32[]{:T(128)}, f32[4,4,128,128]{3,2,1,0:T(8,128)S(1)}, s32[]{:T(128)}, f32[32,4,4,128,128]{4,3,2,1,0:T(8,128)}, s32[]{:T(128)}, ...), condition=%wide.region_4.5_spmd.clone, body=%wide.region_3.4_spmd.clone.sunk | while | flops 786436 | bytes 3145821 | solution.py:33
  424.5 1.7 add_select_fusion.2
  426.2 1.6 add_select_fusion.2
  427.9 1.6 add_select_fusion.2
  429.5 1.6 add_select_fusion.2
  431.1 1.6 add_select_fusion.2
  432.7 1.6 add_select_fusion.2
  434.3 1.6 add_select_fusion.2
  435.9 1.6 add_select_fusion.2
  437.5 1.6 add_select_fusion.2
  439.1 1.6 add_select_fusion.2
  440.8 1.6 add_select_fusion.2
  442.4 1.6 add_select_fusion.2
  444.0 1.6 add_select_fusion.2
  445.6 1.6 add_select_fusion.2
  447.2 1.6 add_select_fusion.2
  448.8 1.6 add_select_fusion.2
  450.4 1.6 add_select_fusion.2
  452.1 1.6 add_select_fusion.2
  453.7 1.6 add_select_fusion.2
  455.3 1.6 add_select_fusion.2
  456.9 1.6 add_select_fusion.2
  458.5 1.6 add_select_fusion.2
  460.1 1.6 add_select_fusion.2
  463.4 1.6 add_select_fusion.2
  465.0 1.6 add_select_fusion.2
  466.6 1.6 add_select_fusion.2
  471.4 1.6 add_select_fusion.2
  473.0 1.6 add_select_fusion.2
  474.6 1.6 add_select_fusion.2
  (327 shorter events, 89.5 us)
Async XLA Ops:
  6.5 8.9 %copy-start = (f32[64,32]{0,1:T(8,128)S(1)}, f32[64,32]{0,1:T(8,128)}, u32[]{:S(2)}) copy-start(f32[64,32]{0,1:T(8,128)} %param.16) | copy-start | bytes 24580
  6.5 1.9 copy-start.4
  6.5 227.0 %all-gather.4.cloned.1.call-start = ((), (), s32[]{:S(2)}) async-start(), calls=%async_computation | async-start | bytes 34603008 | tf_op jit(solution)/shard_map/all_gather | solution.py:38
  7.3 8.0 %copy-start.6 = (f32[27,32,4]{1,2,0:T(4,128)S(1)}, f32[27,32,4]{1,2,0:T(4,128)}, u32[]{:S(2)}) copy-start(f32[27,32,4]{1,2,0:T(4,128)} %param.18) | copy-start | bytes 41476
  7.3 8.1 %copy-start.7 = (f32[64]{0:T(128)S(1)}, f32[64]{0:T(128)}, u32[]{:S(2)}) copy-start(f32[64]{0:T(128)} %param.15) | copy-start | bytes 772
  7.3 8.1 %copy-start.8 = (f32[32]{0:T(128)S(1)}, f32[32]{0:T(128)}, u32[]{:S(2)}) copy-start(f32[32]{0:T(128)} %param.17) | copy-start | bytes 388
  8.4 10.1 %copy-start.9 = (f32[4,32]{1,0:T(4,128)S(1)}, f32[4,32]{1,0:T(4,128)}, u32[]{:S(2)}) copy-start(f32[4,32]{1,0:T(4,128)} %param.19) | copy-start | bytes 1540
  8.4 416.1 %all-gather.6.cloned.1.call-start = ((), (), s32[]{:S(2)}) async-start(), calls=%async_computation.1 | async-start | bytes 34603008 | tf_op jit(solution)/shard_map/all_gather | solution.py:25
  8.5 9.8 %collective-permute-start = (f32[1,4,1,128,128]{4,3,2,1,0:T(8,128)S(1)}, f32[1,4,1,128,128]{4,3,2,1,0:T(8,128)S(1)}, u32[]{:S(2)}, u32[]{:S(2)}) collective-permute-start(f32[1,4,1,128,128]{4,3,2,1,0:T(8,128)S(1)} %get-tuple-element.270), channel_id=1, source_target_pairs={{0,1},{1,2},{2,3},{3,4},{4,5},{5,6},{6,7},{7,0},{8,9},{9,10},{10,1... | collective-permute-start | bytes 786440 | tf_op jit(solution)/shard_map/ppermute | solution.py:15
  10.7 7.7 %collective-permute-start.1 = (f32[1,4,1,128,128]{4,3,2,1,0:T(8,128)S(1)}, f32[1,4,1,128,128]{4,3,2,1,0:T(8,128)S(1)}, u32[]{:S(2)}, u32[]{:S(2)}) collective-permute-start(f32[1,4,1,128,128]{4,3,2,1,0:T(8,128)S(1)} %get-tuple-element.271), channel_id=1, source_target_pairs={{1,0},{2,1},{3,2},{4,3},{5,4},{6,5},{7,6},{0,7},{9,8},{10,9},{11,1... | collective-permute-start | bytes 786440 | tf_op jit(solution)/shard_map/ppermute | solution.py:18
  18.5 2.9 copy-start.2
  69.9 2.4 copy-start.3
  72.3 2.9 copy-start.2
  123.6 2.4 copy-start.3
  126.0 2.9 copy-start.2
  177.5 2.4 copy-start.3
  179.9 2.9 copy-start.2
  231.1 2.4 copy-start.3
  424.5 51.7 %copy-start.5 = (f32[4,4,128,128]{3,2,0,1:T(8,128)S(1)}, f32[4,4,128,128]{3,2,0,1:T(8,128)}, u32[]{:S(2)}) copy-start(f32[4,4,128,128]{3,2,0,1:T(8,128)} %get-tuple-element.145) | copy-start | bytes 3145732
  476.3 1.2 copy-start.1
Sparse Core Ops, SparseCore 0:
  9.2 188.4 all-gather.3
  233.6 190.8 all-gather.5
